TPU v7x, 256 devices: a whole 4x4x8 slice. The times are simulated.
256 devices in a mesh: row: 16 (over z, core), col: 16 (over x, y).
Axes of the slice: x: 4, y: 4, z: 8, core: 2. Of those that a mesh axis runs over, the one named last changes fastest.
Arguments:
- gram: float32 [16, 16, 1024, 1024], P('row', 'col'), may hold values from -21834.348 to 21835.348, as said below
Outputs:
- factored: float32 [16, 16, 1024, 1024], P('row', 'col')
Inputs may be any that keep to these rules, and one draw needn't show every extreme that they name: gram holds a symmetric positive definite matrix of order 16384 whose smallest eigenvalue is at least 1.
All inputs are finite; a program needn't handle non-finite values.
Results may differ from a plain program's by a relative error of at most 0.0001.
Values sent between devices are 32-bit elements; how exact they have to be, the bound alone decides.
No kernel may reach another device: no remote copies, remote signals or barrier semaphores. Data moves between devices by JAX's collectives and lax.ppermute only.
A program may use at most 64 MiB of HBM per device.

v0:
```python
import jax
import jax.numpy as jnp
from jax import lax
from jax.sharding import Mesh
from jax.sharding import PartitionSpec as P

BS = 256
PANELS = 3
ROW = ("row_0", "row_1")


def broadcast(shard, axis, root):
    return lax.dynamic_index_in_dim(lax.all_gather(shard, axis), root, 0, keepdims=False)


def spread(shard, axis, root):
    mine = lax.axis_index(axis) == root
    return lax.psum(jnp.where(mine, shard, jnp.zeros_like(shard)), axis)


def rows_for(lines, devices):
    spare = -len(lines) % devices
    return jnp.pad(lines, [(0, spare)] + [(0, 0)] * (lines.ndim - 1))


def own_block(blocks, axes, sequence):
    inside = blocks.shape[1:]
    blocks = blocks.reshape(*(lax.axis_size(a) for a in axes), *inside)
    blocks = jnp.moveaxis(blocks, sequence, range(len(axes))).reshape(-1, *inside)
    for k in sequence:
        blocks = lax.psum_scatter(blocks, axes[k], scatter_dimension=0, tiled=True)
    return blocks[0]


def stacked_from(shard, axes, sequence):
    blocks = shard[None]
    for k in sequence:
        blocks = lax.all_gather(blocks, axes[k], axis=0, tiled=True)
    current = [lax.axis_size(axes[k]) for k in reversed(sequence)]
    blocks = blocks.reshape(*current, *shard.shape)
    turned = sorted(range(len(sequence)), key=lambda place: sequence[len(sequence) - 1 - place])
    return blocks.transpose(*turned, *range(len(sequence), blocks.ndim)).reshape(-1, *shard.shape)


def total_of(shard, axes, sequence):
    devices, lines = (lax.axis_size(axes), shard.reshape(-1, *shard.shape[1:][-1:]))
    blocks = rows_for(lines, devices).reshape(devices, -1, *lines.shape[1:])
    own = own_block(blocks, axes, sequence)
    whole = stacked_from(own, axes, sequence[::-1]).reshape(-1, *lines.shape[1:])
    return whole[: len(lines)].reshape(shard.shape)


def full_dot(left, right):
    return jnp.dot(
        left, right.T, precision=lax.Precision.HIGHEST, preferred_element_type=jnp.float32
    )


def on_device(gram):
    matrix = gram[0, 0]
    grid_rows = lax.axis_size(ROW)
    grid_cols = lax.axis_size("col")
    own_row = lax.axis_index(ROW)
    own_col = lax.axis_index("col")
    row_count = matrix.shape[0] // BS
    col_count = matrix.shape[1] // BS
    row_blocks = jnp.repeat(jnp.arange(row_count, dtype=jnp.int32) * grid_rows + own_row, BS)
    col_blocks = jnp.repeat(jnp.arange(col_count, dtype=jnp.int32) * grid_cols + own_col, BS)
    for step in range(PANELS):
        first = step // grid_cols * BS
        column = matrix[:, first : first + BS]
        factor_first = step // grid_rows * BS
        corner = broadcast(column[factor_first : factor_first + BS], ROW, step % grid_rows)
        holder = own_col == step % grid_cols
        corner = jnp.where(holder, corner, jnp.eye(BS, dtype=jnp.float32))
        diagonal = jnp.linalg.cholesky(corner)
        solved = lax.linalg.triangular_solve(
            diagonal, column, left_side=False, lower=True, transpose_a=True
        )
        tiled = jnp.tile(diagonal, (row_count, 1))
        result = jnp.where((row_blocks == step)[:, None], tiled, solved)
        result = jnp.where((row_blocks < step)[:, None], jnp.zeros_like(result), result)
        panel_rows = spread(result, "col", step % grid_cols)
        wanted = jnp.arange(col_count, dtype=jnp.int32)[:, None] * grid_cols + own_col
        summed_present = jnp.arange(row_count, dtype=jnp.int32)[None, :] * grid_rows + own_row
        select = (wanted == summed_present).astype(jnp.float32)
        pieces = jnp.einsum(
            "ci,irs->crs",
            select,
            panel_rows.reshape(row_count, BS, BS),
            precision=lax.Precision.HIGHEST,
        )
        panel_cols = total_of(pieces.reshape(col_count * BS, BS), ROW, (0, 1))
        left = jnp.where((row_blocks > step)[:, None], panel_rows, jnp.zeros_like(panel_rows))
        right = jnp.where((col_blocks > step)[:, None], panel_cols, jnp.zeros_like(panel_cols))
        current = matrix - full_dot(left, right)
        finish_first = step // grid_cols * BS
        present = current[:, finish_first : finish_first + BS]
        current = current.at[:, finish_first : finish_first + BS].set(
            jnp.where(own_col == step % grid_cols, panel_rows, present)
        )
        cleared = (row_blocks == step)[:, None] & (col_blocks > step)[None, :]
        matrix = jnp.where(cleared, jnp.zeros_like(current), current)
    return matrix[None, None]


def solution(mesh):
    split = Mesh(mesh.devices.reshape(8, 2, mesh.shape["col"]), ("row_0", "row_1", "col"))
    return jax.shard_map(
        on_device,
        mesh=split,
        in_specs=(P(ROW, "col", None, None),),
        out_specs=P(ROW, "col", None, None),
        check_vma=False,
    )
```

profile of v0, /device:TPU:2, one launch (start us, length us, event | category | flops | bytes accessed | tf_op | source)
XLA Modules:
  0.0 979.8 jit_solution(14150500300622532511)
XLA Ops:
  6.5 5.3 copy.36
  13.8 45.0 %all-gather.16.cloned.1.call-done = f32[4096,256]{0,1:T(8,128)} async-done(((f32[256,256]{0,1:T(8,128)}), f32[4096,256]{0,1:T(8,128)}) %all-gather.16.cloned.1.call-update) | async-done | bytes 4194320 | tf_op jit(solution)/shard_map/all_gather | solution.py:13
  60.9 11.7 %cholesky.172 = f32[128,128]{1,0:T(8,128)S(1)} custom-call(f32[128,128]{1,0:T(8,128)S(1)} %cholesky.270), custom_call_target="Cholesky" | custom-call | tf_op jit(solution)/shard_map/jit(cholesky)/cholesky | solution.py:76
  72.7 9.8 %custom-call.15 = f32[1,128,128]{1,2,0:T(8,128)S(1)} custom-call(f32[1,128,128]{2,1,0:T(8,128)S(1)} %get-tuple-element.113), custom_call_target="InvertDiagBlocksLowerTriangular" | custom-call | tf_op jit(solution)/shard_map/jit(cholesky)/cholesky | solution.py:76
  83.0 11.7 %cholesky.189 = f32[128,128]{1,0:T(8,128)S(1)} custom-call(f32[128,128]{1,0:T(8,128)S(1)} %convolution_subtract_fusion.8), custom_call_target="Cholesky" | custom-call | tf_op jit(solution)/shard_map/jit(cholesky)/cholesky | solution.py:76
  101.3 19.7 %custom-call.16 = f32[2,128,128]{1,2,0:T(8,128)S(1)} custom-call(f32[2,128,128]{2,1,0:T(8,128)S(1)} %get-tuple-element.63), custom_call_target="InvertDiagBlocksLowerTriangular" | custom-call | tf_op jit(solution)/shard_map/triangular_solve/custom-call.0 | solution.py:77
  126.8 95.4 %all-reduce.5.cloned.1.call-done = f32[1024,256]{0,1:T(8,128)} async-done(((f32[1024,256]{0,1:T(8,128)}), f32[1024,256]{0,1:T(8,128)}) %all-reduce.5.cloned.1.call-update) | async-done | bytes 1048592 | tf_op jit(solution)/shard_map/psum | solution.py:18
  227.0 38.5 %reduce-scatter.7.cloned.1.call-done = f32[2,64,256]{2,1,0:T(8,128)} async-done(((f32[16,64,256]{2,1,0:T(8,128)}), f32[2,64,256]{2,1,0:T(8,128)}) %reduce-scatter.7.cloned.1.call-update) | async-done | bytes 131088 | tf_op jit(solution)/shard_map/reduce_scatter | solution.py:31
  265.6 13.8 %reduce-scatter.9.cloned.1.call-done = f32[1,64,256]{2,1,0:T(8,128)} async-done(((f32[2,64,256]{2,1,0:T(8,128)}), f32[1,64,256]{2,1,0:T(8,128)}) %reduce-scatter.9.cloned.1.call-update) | async-done | bytes 65552 | tf_op jit(solution)/shard_map/reduce_scatter | solution.py:31
  283.8 39.3 %all-gather.10.cloned.1.call-done = f32[16,64,256]{2,1,0:T(8,128)} async-done(((f32[2,64,256]{2,1,0:T(8,128)}), f32[16,64,256]{2,1,0:T(8,128)}) %all-gather.10.cloned.1.call-update) | async-done | bytes 1048592 | tf_op jit(solution)/shard_map/all_gather | solution.py:38
  324.7 5.5 convolution_subtract_fusion.2
  335.0 40.1 %all-gather.18.cloned.1.call-done = f32[4096,256]{0,1:T(8,128)} async-done(((f32[256,256]{0,1:T(8,128)}), f32[4096,256]{0,1:T(8,128)}) %all-gather.18.cloned.1.call-update) | async-done | bytes 4194320 | tf_op jit(solution)/shard_map/all_gather | solution.py:13
  377.2 11.7 %cholesky.206 = f32[128,128]{1,0:T(8,128)S(1)} custom-call(f32[128,128]{1,0:T(8,128)S(1)} %cholesky.273), custom_call_target="Cholesky" | custom-call | tf_op jit(solution)/shard_map/jit(cholesky)/cholesky | solution.py:76
  389.0 9.8 %custom-call.17 = f32[1,128,128]{1,2,0:T(8,128)S(1)} custom-call(f32[1,128,128]{2,1,0:T(8,128)S(1)} %get-tuple-element.109), custom_call_target="InvertDiagBlocksLowerTriangular" | custom-call | tf_op jit(solution)/shard_map/jit(cholesky)/cholesky | solution.py:76
  399.3 11.7 %cholesky.223 = f32[128,128]{1,0:T(8,128)S(1)} custom-call(f32[128,128]{1,0:T(8,128)S(1)} %convolution_subtract_fusion.7), custom_call_target="Cholesky" | custom-call | tf_op jit(solution)/shard_map/jit(cholesky)/cholesky | solution.py:76
  418.2 19.7 %custom-call.18 = f32[2,128,128]{1,2,0:T(8,128)S(1)} custom-call(f32[2,128,128]{2,1,0:T(8,128)S(1)} %get-tuple-element.64), custom_call_target="InvertDiagBlocksLowerTriangular" | custom-call | tf_op jit(solution)/shard_map/triangular_solve/custom-call.0 | solution.py:77
  443.6 95.4 %all-reduce.7.cloned.1.call-done = f32[1024,256]{0,1:T(8,128)} async-done(((f32[1024,256]{0,1:T(8,128)}), f32[1024,256]{0,1:T(8,128)}) %all-reduce.7.cloned.1.call-update) | async-done | bytes 1048592 | tf_op jit(solution)/shard_map/psum | solution.py:18
  543.9 38.5 %reduce-scatter.11.cloned.1.call-done = f32[2,64,256]{2,1,0:T(8,128)} async-done(((f32[16,64,256]{2,1,0:T(8,128)}), f32[2,64,256]{2,1,0:T(8,128)}) %reduce-scatter.11.cloned.1.call-update) | async-done | bytes 131088 | tf_op jit(solution)/shard_map/reduce_scatter | solution.py:31
  582.4 14.0 %reduce-scatter.13.cloned.1.call-done = f32[1,64,256]{2,1,0:T(8,128)} async-done(((f32[2,64,256]{2,1,0:T(8,128)}), f32[1,64,256]{2,1,0:T(8,128)}) %reduce-scatter.13.cloned.1.call-update) | async-done | bytes 65552 | tf_op jit(solution)/shard_map/reduce_scatter | solution.py:31
  600.2 39.9 %all-gather.12.cloned.1.call-done = f32[16,64,256]{2,1,0:T(8,128)} async-done(((f32[2,64,256]{2,1,0:T(8,128)}), f32[16,64,256]{2,1,0:T(8,128)}) %all-gather.12.cloned.1.call-update) | async-done | bytes 1048592 | tf_op jit(solution)/shard_map/all_gather | solution.py:38
  641.7 5.5 convolution_subtract_fusion.1
  651.9 40.3 %all-gather.20.cloned.1.call-done = f32[4096,256]{0,1:T(8,128)} async-done(((f32[256,256]{0,1:T(8,128)}), f32[4096,256]{0,1:T(8,128)}) %all-gather.20.cloned.1.call-update) | async-done | bytes 4194320 | tf_op jit(solution)/shard_map/all_gather | solution.py:13
  694.3 11.7 %cholesky.240 = f32[128,128]{1,0:T(8,128)S(1)} custom-call(f32[128,128]{1,0:T(8,128)S(1)} %cholesky.276), custom_call_target="Cholesky" | custom-call | tf_op jit(solution)/shard_map/jit(cholesky)/cholesky | solution.py:76
  706.0 9.8 %custom-call.19 = f32[1,128,128]{1,2,0:T(8,128)S(1)} custom-call(f32[1,128,128]{2,1,0:T(8,128)S(1)} %get-tuple-element.105), custom_call_target="InvertDiagBlocksLowerTriangular" | custom-call | tf_op jit(solution)/shard_map/jit(cholesky)/cholesky | solution.py:76
  716.3 11.7 %cholesky.257 = f32[128,128]{1,0:T(8,128)S(1)} custom-call(f32[128,128]{1,0:T(8,128)S(1)} %convolution_subtract_fusion.6), custom_call_target="Cholesky" | custom-call | tf_op jit(solution)/shard_map/jit(cholesky)/cholesky | solution.py:76
  735.3 19.7 %custom-call.20 = f32[2,128,128]{1,2,0:T(8,128)S(1)} custom-call(f32[2,128,128]{2,1,0:T(8,128)S(1)} %get-tuple-element.65), custom_call_target="InvertDiagBlocksLowerTriangular" | custom-call | tf_op jit(solution)/shard_map/triangular_solve/custom-call.0 | solution.py:77
  760.8 95.4 %all-reduce.9.cloned.1.call-done = f32[1024,256]{0,1:T(8,128)} async-done(((f32[1024,256]{0,1:T(8,128)}), f32[1024,256]{0,1:T(8,128)}) %all-reduce.9.cloned.1.call-update) | async-done | bytes 1048592 | tf_op jit(solution)/shard_map/psum | solution.py:18
  861.0 38.5 %reduce-scatter.15.cloned.1.call-done = f32[2,64,256]{2,1,0:T(8,128)} async-done(((f32[16,64,256]{2,1,0:T(8,128)}), f32[2,64,256]{2,1,0:T(8,128)}) %reduce-scatter.15.cloned.1.call-update) | async-done | bytes 131088 | tf_op jit(solution)/shard_map/reduce_scatter | solution.py:31
  899.6 13.8 %reduce-scatter.17.cloned.1.call-done = f32[1,64,256]{2,1,0:T(8,128)} async-done(((f32[2,64,256]{2,1,0:T(8,128)}), f32[1,64,256]{2,1,0:T(8,128)}) %reduce-scatter.17.cloned.1.call-update) | async-done | bytes 65552 | tf_op jit(solution)/shard_map/reduce_scatter | solution.py:31
  917.1 40.0 %all-gather.14.cloned.1.call-done = f32[16,64,256]{2,1,0:T(8,128)} async-done(((f32[2,64,256]{2,1,0:T(8,128)}), f32[16,64,256]{2,1,0:T(8,128)}) %all-gather.14.cloned.1.call-update) | async-done | bytes 1048592 | tf_op jit(solution)/shard_map/all_gather | solution.py:38
  958.7 5.5 convolution_subtract_fusion
  967.5 5.3 copy.58
  (183 shorter events, 100.2 us)
Async XLA Ops:
  6.5 52.3 %all-gather.16.cloned.1.call-start = ((), (), s32[]{:S(2)}) async-start(), calls=%async_computation.18 | async-start | bytes 4456448 | tf_op jit(solution)/shard_map/all_gather | solution.py:13
  13.6 208.6 %all-reduce.5.cloned.1.call-start = ((), (), s32[]{:S(2)}) async-start(), calls=%async_computation.6 | async-start | bytes 2097152 | tf_op jit(solution)/shard_map/psum | solution.py:18
  126.7 138.8 %reduce-scatter.7.cloned.1.call-start = ((), (), s32[]{:S(2)}) async-start(), calls=%async_computation.7 | async-start | bytes 1179648 | tf_op jit(solution)/shard_map/reduce_scatter | solution.py:31
  224.6 100.1 %copy-start.2 = (f32[1024,256]{0,1:T(8,128)S(1)}, f32[1024,256]{0,1:T(8,128)}, u32[]{:S(2)}) copy-start(f32[1024,256]{0,1:T(8,128)} %all-reduce.5.cloned.1.call-done) | copy-start | bytes 3145732
  226.9 52.4 %reduce-scatter.9.cloned.1.call-start = ((), (), s32[]{:S(2)}) async-start(), calls=%async_computation.8 | async-start | bytes 196608 | tf_op jit(solution)/shard_map/reduce_scatter | solution.py:31
  265.5 57.6 %all-gather.10.cloned.1.call-start = ((), (), s32[]{:S(2)}) async-start(), calls=%async_computation.9 | async-start | bytes 1179648 | tf_op jit(solution)/shard_map/all_gather | solution.py:38
  282.9 92.2 %all-gather.18.cloned.1.call-start = ((), (), s32[]{:S(2)}) async-start(), calls=%async_computation.19 | async-start | bytes 4456448 | tf_op jit(solution)/shard_map/all_gather | solution.py:13
  331.6 2.0 copy-start.1
  334.3 204.7 %all-reduce.7.cloned.1.call-start = ((), (), s32[]{:S(2)}) async-start(), calls=%async_computation.10 | async-start | bytes 2097152 | tf_op jit(solution)/shard_map/psum | solution.py:18
  443.6 138.8 %reduce-scatter.11.cloned.1.call-start = ((), (), s32[]{:S(2)}) async-start(), calls=%async_computation.11 | async-start | bytes 1179648 | tf_op jit(solution)/shard_map/reduce_scatter | solution.py:31
  541.4 100.3 %copy-start.4 = (f32[1024,256]{0,1:T(8,128)S(1)}, f32[1024,256]{0,1:T(8,128)}, u32[]{:S(2)}) copy-start(f32[1024,256]{0,1:T(8,128)} %all-reduce.7.cloned.1.call-done) | copy-start | bytes 3145732
  543.8 52.6 %reduce-scatter.13.cloned.1.call-start = ((), (), s32[]{:S(2)}) async-start(), calls=%async_computation.12 | async-start | bytes 196608 | tf_op jit(solution)/shard_map/reduce_scatter | solution.py:31
  582.4 57.8 %all-gather.12.cloned.1.call-start = ((), (), s32[]{:S(2)}) async-start(), calls=%async_computation.13 | async-start | bytes 1179648 | tf_op jit(solution)/shard_map/all_gather | solution.py:38
  600.0 92.2 %all-gather.20.cloned.1.call-start = ((), (), s32[]{:S(2)}) async-start(), calls=%async_computation.20 | async-start | bytes 4456448 | tf_op jit(solution)/shard_map/all_gather | solution.py:13
  648.6 2.0 copy-start
  651.4 204.8 %all-reduce.9.cloned.1.call-start = ((), (), s32[]{:S(2)}) async-start(), calls=%async_computation.14 | async-start | bytes 2097152 | tf_op jit(solution)/shard_map/psum | solution.py:18
  760.7 138.8 %reduce-scatter.15.cloned.1.call-start = ((), (), s32[]{:S(2)}) async-start(), calls=%async_computation.15 | async-start | bytes 1179648 | tf_op jit(solution)/shard_map/reduce_scatter | solution.py:31
  858.6 100.1 %copy-start.3 = (f32[1024,256]{0,1:T(8,128)S(1)}, f32[1024,256]{0,1:T(8,128)}, u32[]{:S(2)}) copy-start(f32[1024,256]{0,1:T(8,128)} %all-reduce.9.cloned.1.call-done) | copy-start | bytes 3145732
  861.0 52.5 %reduce-scatter.17.cloned.1.call-start = ((), (), s32[]{:S(2)}) async-start(), calls=%async_computation.16 | async-start | bytes 196608 | tf_op jit(solution)/shard_map/reduce_scatter | solution.py:31
  899.5 57.6 %all-gather.14.cloned.1.call-start = ((), (), s32[]{:S(2)}) async-start(), calls=%async_computation.17 | async-start | bytes 1179648 | tf_op jit(solution)/shard_map/all_gather | solution.py:38
Sparse Core Ops, SparseCore 0:
  13.7 45.0 all-gather.15
  126.8 95.2 all-reduce.4
  227.1 38.3 reduce-scatter.6
  267.8 11.5 reduce-scatter.8
  283.0 39.9 all-gather.9
  334.5 40.5 all-gather.17
  443.7 95.2 all-reduce.6
  543.9 38.3 reduce-scatter.10
  584.8 11.5 reduce-scatter.12
  600.1 39.9 all-gather.11
  651.5 40.5 all-gather.19
  760.8 95.2 all-reduce.8
  861.1 38.3 reduce-scatter.14
  901.8 11.5 reduce-scatter.16
  917.1 39.9 all-gather.13
where the time goes:
time: 989 us; the launch traced here: 980 us
  waiting for transfers between devices  688 us (70%)
  other arithmetic  179 us (18%)
  local copies, waits for them, and re-layouts  48.8 us (5%)
  matrix products  33 us (3%)
  between operations  18.3 us (2%)
  blocking collectives  10.6 us (1%)
    psum x3, waiting for transfers between devices, spread(): return lax.psum(jnp.where(mine, shard, jnp.zeros_like(shard)), axis)  286 us
    reduce_scatter x6, waiting for transfers between devices, own_block(): blocks = lax.psum_scatter(blocks, axes[k], scatter_dimension=0, tiled=True)  157 us
    all_gather x3, waiting for transfers between devices, broadcast(): lax.all_gather(shard, axis)  125 us
    all_gather x3, waiting for transfers between devices, stacked_from(): blocks = lax.all_gather(blocks, axes[k], axis=0, tiled=True)  119 us
    another operation x20, other arithmetic, on_device(): diagonal = jnp.linalg.cholesky(corner)  103 us
    another operation x7, other arithmetic, on_device(): lax.linalg.triangular_solve(diagonal, column, left_side=False, lower=True...  59.1 us
  transfers between devices with their start and end apart: 15, of which 15 were waited for; matrix products, arithmetic and copies ran while one was open for 0% of the time, Pallas kernels for 0%

commit v1 on v0

--- a/solution.py
+++ b/solution.py
@@ -3,6 +3,7 @@
 from jax import lax
 from jax.sharding import Mesh
 from jax.sharding import PartitionSpec as P
+from jax.lax import all_gather
 
 BS = 256
 PANELS = 3
@@ -15,7 +16,11 @@
 
 def spread(shard, axis, root):
     mine = lax.axis_index(axis) == root
-    return lax.psum(jnp.where(mine, shard, jnp.zeros_like(shard)), axis)
+
+    def mark_heads_on_mesh(raw, which_axis):
+        return jnp.sum(all_gather(raw, which_axis), axis=0)
+
+    return mark_heads_on_mesh(jnp.where(mine, shard, jnp.zeros_like(shard)), axis)
 
 
 def rows_for(lines, devices):

time: 989 us -> 1130 us (1.14)
  waiting for transfers between devices: 688 us -> 747 us
  local copies, waits for them, and re-layouts: 48.8 us -> 99.7 us
  other arithmetic: 179 us -> 208 us
    all_gather x0 -> x3, waiting for transfers between devices: none -> 345 us  [mark_heads_on_mesh(): return jnp.sum(all_gather(raw, which_axis), axis=0)]
    psum x3 -> x0, waiting for transfers between devices: 286 us -> none  [spread(): return lax.psum(jnp.where(mine, shard, jnp.zeros_like(shard)), axis)]
    unnamed x14 -> x11, local copies, waits for them, and re-layouts: 9.96 us -> 65.8 us
    reduce_sum x0 -> x3, other arithmetic: none -> 29.5 us  [mark_heads_on_mesh(): return jnp.sum(all_gather(raw, which_axis), axis=0)]
where the time goes in v1:
time: 1130 us; the launch traced here: 1120 us
  waiting for transfers between devices  747 us (66%)
  other arithmetic  208 us (18%)
  local copies, waits for them, and re-layouts  99.7 us (9%)
  matrix products  33.4 us (3%)
  between operations  17.9 us (2%)
    all_gather x3, waiting for transfers between devices, mark_heads_on_mesh(): return jnp.sum(all_gather(raw, which_axis), axis=0)  345 us
    reduce_scatter x6, waiting for transfers between devices, own_block(): blocks = lax.psum_scatter(blocks, axes[k], scatter_dimension=0, tiled=True)  157 us
    all_gather x3, waiting for transfers between devices, broadcast(): lax.all_gather(shard, axis)  126 us
    all_gather x3, waiting for transfers between devices, stacked_from(): blocks = lax.all_gather(blocks, axes[k], axis=0, tiled=True)  119 us
    another operation x20, other arithmetic, on_device(): diagonal = jnp.linalg.cholesky(corner)  103 us
    unnamed x11, local copies, waits for them, and re-layouts  65.8 us
    another operation x7, other arithmetic, on_device(): lax.linalg.triangular_solve(diagonal, column, left_side=False, lower=True...  59.1 us
    reduce_sum x3, other arithmetic, mark_heads_on_mesh(): return jnp.sum(all_gather(raw, which_axis), axis=0)  29.5 us
  transfers between devices with their start and end apart: 15, of which 15 were waited for; matrix products, arithmetic and copies ran while one was open for 0% of the time, Pallas kernels for 0%

profile of v1, /device:TPU:2, one launch (start us, length us, event | category | flops | bytes accessed | tf_op | source)
XLA Modules:
  0.0 1118.7 jit_solution(8118023325755052082)
XLA Ops:
  13.8 45.0 %all-gather.22.cloned.1.call-done = f32[4096,256]{0,1:T(8,128)} async-done(((f32[256,256]{0,1:T(8,128)}), f32[4096,256]{0,1:T(8,128)}) %all-gather.22.cloned.1.call-update) | async-done | bytes 4194320 | tf_op jit(solution)/shard_map/all_gather | solution.py:14
  60.9 11.7 %cholesky.172 = f32[128,128]{1,0:T(8,128)S(1)} custom-call(f32[128,128]{1,0:T(8,128)S(1)} %cholesky.270), custom_call_target="Cholesky" | custom-call | tf_op jit(solution)/shard_map/jit(cholesky)/cholesky | solution.py:81
  72.7 9.8 custom-call.15
  83.0 11.7 %cholesky.189 = f32[128,128]{1,0:T(8,128)S(1)} custom-call(f32[128,128]{1,0:T(8,128)S(1)} %convolution_subtract_fusion.8), custom_call_target="Cholesky" | custom-call | tf_op jit(solution)/shard_map/jit(cholesky)/cholesky | solution.py:81
  100.8 19.7 %custom-call.16 = f32[2,128,128]{1,2,0:T(8,128)S(1)} custom-call(f32[2,128,128]{2,1,0:T(8,128)S(1)} %get-tuple-element.63), custom_call_target="InvertDiagBlocksLowerTriangular" | custom-call | tf_op jit(solution)/shard_map/triangular_solve/custom-call.0 | solution.py:82
  126.3 115.0 %all-gather.24.cloned.1.call-done = f32[16384,256]{0,1:T(8,128)} async-done(((f32[1024,256]{0,1:T(8,128)}), f32[16384,256]{0,1:T(8,128)}) %all-gather.24.cloned.1.call-update) | async-done | bytes 16777232 | tf_op jit(solution)/shard_map/all_gather | solution.py:21
  241.3 18.6 %copy.66 = f32[32,8,16,1024]{3,2,1,0:T(8,128)} copy(f32[32,8,16,1024]{3,1,2,0:T(8,128)} %bitcast.152) | data formatting | bytes 33554432
  259.9 9.8 bitcast_reduce_fusion.2
  273.3 38.5 %reduce-scatter.7.cloned.1.call-done = f32[2,64,256]{2,1,0:T(8,128)} async-done(((f32[16,64,256]{2,1,0:T(8,128)}), f32[2,64,256]{2,1,0:T(8,128)}) %reduce-scatter.7.cloned.1.call-update) | async-done | bytes 131088 | tf_op jit(solution)/shard_map/reduce_scatter | solution.py:36
  311.8 13.9 %reduce-scatter.9.cloned.1.call-done = f32[1,64,256]{2,1,0:T(8,128)} async-done(((f32[2,64,256]{2,1,0:T(8,128)}), f32[1,64,256]{2,1,0:T(8,128)}) %reduce-scatter.9.cloned.1.call-update) | async-done | bytes 65552 | tf_op jit(solution)/shard_map/reduce_scatter | solution.py:36
  330.1 39.3 %all-gather.16.cloned.1.call-done = f32[16,64,256]{2,1,0:T(8,128)} async-done(((f32[2,64,256]{2,1,0:T(8,128)}), f32[16,64,256]{2,1,0:T(8,128)}) %all-gather.16.cloned.1.call-update) | async-done | bytes 1048592 | tf_op jit(solution)/shard_map/all_gather | solution.py:43
  381.0 40.3 %all-gather.26.cloned.1.call-done = f32[4096,256]{0,1:T(8,128)} async-done(((f32[256,256]{0,1:T(8,128)}), f32[4096,256]{0,1:T(8,128)}) %all-gather.26.cloned.1.call-update) | async-done | bytes 4194320 | tf_op jit(solution)/shard_map/all_gather | solution.py:14
  423.4 11.7 %cholesky.206 = f32[128,128]{1,0:T(8,128)S(1)} custom-call(f32[128,128]{1,0:T(8,128)S(1)} %cholesky.273), custom_call_target="Cholesky" | custom-call | tf_op jit(solution)/shard_map/jit(cholesky)/cholesky | solution.py:81
  435.2 9.8 custom-call.17
  445.5 11.7 %cholesky.223 = f32[128,128]{1,0:T(8,128)S(1)} custom-call(f32[128,128]{1,0:T(8,128)S(1)} %convolution_subtract_fusion.7), custom_call_target="Cholesky" | custom-call | tf_op jit(solution)/shard_map/jit(cholesky)/cholesky | solution.py:81
  464.0 19.7 %custom-call.18 = f32[2,128,128]{1,2,0:T(8,128)S(1)} custom-call(f32[2,128,128]{2,1,0:T(8,128)S(1)} %get-tuple-element.64), custom_call_target="InvertDiagBlocksLowerTriangular" | custom-call | tf_op jit(solution)/shard_map/triangular_solve/custom-call.0 | solution.py:82
  489.4 115.0 %all-gather.28.cloned.1.call-done = f32[16384,256]{0,1:T(8,128)} async-done(((f32[1024,256]{0,1:T(8,128)}), f32[16384,256]{0,1:T(8,128)}) %all-gather.28.cloned.1.call-update) | async-done | bytes 16777232 | tf_op jit(solution)/shard_map/all_gather | solution.py:21
  604.4 18.6 %copy.68 = f32[32,8,16,1024]{3,2,1,0:T(8,128)} copy(f32[32,8,16,1024]{3,1,2,0:T(8,128)} %bitcast.153) | data formatting | bytes 33554432
  623.0 9.8 bitcast_reduce_fusion.1
  636.4 38.5 %reduce-scatter.11.cloned.1.call-done = f32[2,64,256]{2,1,0:T(8,128)} async-done(((f32[16,64,256]{2,1,0:T(8,128)}), f32[2,64,256]{2,1,0:T(8,128)}) %reduce-scatter.11.cloned.1.call-update) | async-done | bytes 131088 | tf_op jit(solution)/shard_map/reduce_scatter | solution.py:36
  675.0 14.0 %reduce-scatter.13.cloned.1.call-done = f32[1,64,256]{2,1,0:T(8,128)} async-done(((f32[2,64,256]{2,1,0:T(8,128)}), f32[1,64,256]{2,1,0:T(8,128)}) %reduce-scatter.13.cloned.1.call-update) | async-done | bytes 65552 | tf_op jit(solution)/shard_map/reduce_scatter | solution.py:36
  692.7 39.9 %all-gather.18.cloned.1.call-done = f32[16,64,256]{2,1,0:T(8,128)} async-done(((f32[2,64,256]{2,1,0:T(8,128)}), f32[16,64,256]{2,1,0:T(8,128)}) %all-gather.18.cloned.1.call-update) | async-done | bytes 1048592 | tf_op jit(solution)/shard_map/all_gather | solution.py:43
  744.3 40.5 %all-gather.30.cloned.1.call-done = f32[4096,256]{0,1:T(8,128)} async-done(((f32[256,256]{0,1:T(8,128)}), f32[4096,256]{0,1:T(8,128)}) %all-gather.30.cloned.1.call-update) | async-done | bytes 4194320 | tf_op jit(solution)/shard_map/all_gather | solution.py:14
  786.9 11.7 %cholesky.240 = f32[128,128]{1,0:T(8,128)S(1)} custom-call(f32[128,128]{1,0:T(8,128)S(1)} %cholesky.276), custom_call_target="Cholesky" | custom-call | tf_op jit(solution)/shard_map/jit(cholesky)/cholesky | solution.py:81
  809.0 11.7 %cholesky.257 = f32[128,128]{1,0:T(8,128)S(1)} custom-call(f32[128,128]{1,0:T(8,128)S(1)} %convolution_subtract_fusion.6), custom_call_target="Cholesky" | custom-call | tf_op jit(solution)/shard_map/jit(cholesky)/cholesky | solution.py:81
  827.2 19.7 %custom-call.20 = f32[2,128,128]{1,2,0:T(8,128)S(1)} custom-call(f32[2,128,128]{2,1,0:T(8,128)S(1)} %get-tuple-element.65), custom_call_target="InvertDiagBlocksLowerTriangular" | custom-call | tf_op jit(solution)/shard_map/triangular_solve/custom-call.0 | solution.py:82
  852.7 115.0 %all-gather.32.cloned.1.call-done = f32[16384,256]{0,1:T(8,128)} async-done(((f32[1024,256]{0,1:T(8,128)}), f32[16384,256]{0,1:T(8,128)}) %all-gather.32.cloned.1.call-update) | async-done | bytes 16777232 | tf_op jit(solution)/shard_map/all_gather | solution.py:21
  967.6 18.6 %copy.70 = f32[32,8,16,1024]{3,2,1,0:T(8,128)} copy(f32[32,8,16,1024]{3,1,2,0:T(8,128)} %bitcast.154) | data formatting | bytes 33554432
  986.3 9.8 bitcast_reduce_fusion
  999.6 38.5 %reduce-scatter.15.cloned.1.call-done = f32[2,64,256]{2,1,0:T(8,128)} async-done(((f32[16,64,256]{2,1,0:T(8,128)}), f32[2,64,256]{2,1,0:T(8,128)}) %reduce-scatter.15.cloned.1.call-update) | async-done | bytes 131088 | tf_op jit(solution)/shard_map/reduce_scatter | solution.py:36
  1038.2 13.9 %reduce-scatter.17.cloned.1.call-done = f32[1,64,256]{2,1,0:T(8,128)} async-done(((f32[2,64,256]{2,1,0:T(8,128)}), f32[1,64,256]{2,1,0:T(8,128)}) %reduce-scatter.17.cloned.1.call-update) | async-done | bytes 65552 | tf_op jit(solution)/shard_map/reduce_scatter | solution.py:36
  1055.8 40.0 %all-gather.20.cloned.1.call-done = f32[16,64,256]{2,1,0:T(8,128)} async-done(((f32[2,64,256]{2,1,0:T(8,128)}), f32[16,64,256]{2,1,0:T(8,128)}) %all-gather.20.cloned.1.call-update) | async-done | bytes 1048592 | tf_op jit(solution)/shard_map/all_gather | solution.py:43
  (184 shorter events, 130.5 us)
Async XLA Ops:
  6.5 52.3 %all-gather.22.cloned.1.call-start = ((), (), s32[]{:S(2)}) async-start(), calls=%async_computation.15 | async-start | bytes 4456448 | tf_op jit(solution)/shard_map/all_gather | solution.py:14
  13.6 227.7 %all-gather.24.cloned.1.call-start = ((), (), s32[]{:S(2)}) async-start(), calls=%async_computation.16 | async-start | bytes 17825792 | tf_op jit(solution)/shard_map/all_gather | solution.py:21
  126.2 185.5 %reduce-scatter.7.cloned.1.call-start = ((), (), s32[]{:S(2)}) async-start(), calls=%async_computation.6 | async-start | bytes 1179648 | tf_op jit(solution)/shard_map/reduce_scatter | solution.py:36
  273.2 52.5 %reduce-scatter.9.cloned.1.call-start = ((), (), s32[]{:S(2)}) async-start(), calls=%async_computation.7 | async-start | bytes 196608 | tf_op jit(solution)/shard_map/reduce_scatter | solution.py:36
  311.8 57.6 %all-gather.16.cloned.1.call-start = ((), (), s32[]{:S(2)}) async-start(), calls=%async_computation.8 | async-start | bytes 1179648 | tf_op jit(solution)/shard_map/all_gather | solution.py:43
  329.2 92.1 %all-gather.26.cloned.1.call-start = ((), (), s32[]{:S(2)}) async-start(), calls=%async_computation.17 | async-start | bytes 4456448 | tf_op jit(solution)/shard_map/all_gather | solution.py:14
  377.8 2.0 copy-start.1
  380.5 223.8 %all-gather.28.cloned.1.call-start = ((), (), s32[]{:S(2)}) async-start(), calls=%async_computation.18 | async-start | bytes 17825792 | tf_op jit(solution)/shard_map/all_gather | solution.py:21
  489.4 185.5 %reduce-scatter.11.cloned.1.call-start = ((), (), s32[]{:S(2)}) async-start(), calls=%async_computation.9 | async-start | bytes 1179648 | tf_op jit(solution)/shard_map/reduce_scatter | solution.py:36
  636.3 52.6 %reduce-scatter.13.cloned.1.call-start = ((), (), s32[]{:S(2)}) async-start(), calls=%async_computation.10 | async-start | bytes 196608 | tf_op jit(solution)/shard_map/reduce_scatter | solution.py:36
  674.9 57.8 %all-gather.18.cloned.1.call-start = ((), (), s32[]{:S(2)}) async-start(), calls=%async_computation.11 | async-start | bytes 1179648 | tf_op jit(solution)/shard_map/all_gather | solution.py:43
  692.5 92.3 %all-gather.30.cloned.1.call-start = ((), (), s32[]{:S(2)}) async-start(), calls=%async_computation.19 | async-start | bytes 4456448 | tf_op jit(solution)/shard_map/all_gather | solution.py:14
  741.2 2.0 copy-start
  744.0 223.6 %all-gather.32.cloned.1.call-start = ((), (), s32[]{:S(2)}) async-start(), calls=%async_computation.20 | async-start | bytes 17825792 | tf_op jit(solution)/shard_map/all_gather | solution.py:21
  852.6 185.5 %reduce-scatter.15.cloned.1.call-start = ((), (), s32[]{:S(2)}) async-start(), calls=%async_computation.12 | async-start | bytes 1179648 | tf_op jit(solution)/shard_map/reduce_scatter | solution.py:36
  999.6 52.5 %reduce-scatter.17.cloned.1.call-start = ((), (), s32[]{:S(2)}) async-start(), calls=%async_computation.13 | async-start | bytes 196608 | tf_op jit(solution)/shard_map/reduce_scatter | solution.py:36
  1038.2 57.6 %all-gather.20.cloned.1.call-start = ((), (), s32[]{:S(2)}) async-start(), calls=%async_computation.14 | async-start | bytes 1179648 | tf_op jit(solution)/shard_map/all_gather | solution.py:43
Sparse Core Ops, SparseCore 0:
  13.7 45.0 all-gather.21
  126.3 114.8 all-gather.23
  273.3 38.3 reduce-scatter.6
  314.1 11.5 reduce-scatter.8
  329.3 40.0 all-gather.15
  380.7 40.5 all-gather.25
  489.5 114.8 all-gather.27
  636.5 38.3 reduce-scatter.10
  677.3 11.5 reduce-scatter.12
  692.6 40.0 all-gather.17
  744.1 40.5 all-gather.29
  852.7 114.8 all-gather.31
  999.7 38.3 reduce-scatter.14
  1040.5 11.5 reduce-scatter.16
  1055.7 40.0 all-gather.19
